TPU v7x, 32 devices: a whole 2x2x4 slice. The times are simulated.
32 devices in a mesh: groups: 2 (over y), seq: 4 (over z), head: 2 (over x), cache: 2 (over core).
Axes of the slice: x: 2, y: 2, z: 4, core: 2. Of those that a mesh axis runs over, the one named last changes fastest.
Arguments:
- head_values: bfloat16 [2, 4096, 8192], P('groups', 'seq', ('head', 'cache')), parts along dimension 0, may hold values from -6 to 6
- gate_values: bfloat16 [2, 4096, 8192], P('groups', 'seq', ('head', 'cache')), parts along dimension 0, may hold values from -6 to 6
- state_inputs: bfloat16 [2, 4096, 8, 128], P('groups', 'seq', 'head'), parts along dimension 0, may hold values from -0.119628906 to 0.119628906
- state_readout: bfloat16 [2, 4096, 8, 128], P('groups', 'seq', 'head'), parts along dimension 0, may hold values from -6 to 6
- log_decays: float32 [2, 4096, 128], P('groups', 'seq', ('head', 'cache')), parts along dimension 0, may hold values from -1 to 0, as said below
- skip_gains: float32 [128], P(('head', 'cache')), may hold values from 0.5 to 2
- norm_gains: float32 [8192], P(('head', 'cache')), may hold values from 0.5 to 1.5
- cached_states: float32 [16, 128, 64, 128], P(('groups', 'seq'), ('head', 'cache')), parts along dimension 0, may hold values from -3 to 3
- owner_slots: int32 [16], P('groups'), parts along dimension 0, may hold values from 0 to 7, each once
- prefix_blocks: int32 [16], P('groups'), parts along dimension 0, may hold values from 1 to 3
- prompt_sessions: int32 [2], P('groups'), parts along dimension 0, may hold values from 0 to 7
Outputs:
- layer_output: bfloat16 [2, 4096, 8192], P('groups', 'seq', ('head', 'cache')), parts along dimension 0
There are 2 independent parts, one for each index of `groups`. A program takes and returns all parts, laid end to end along the dimension named above; an argument that names none is the same for every part. Nothing has to cross between parts.
Inputs may be any that keep to these rules, and one draw needn't show every extreme that they name: owner_slots is a permutation of 0 to 7. `log_decays`: every entry is negative.
All inputs are finite; a program needn't handle non-finite values.
Results may differ from a plain program's by a relative error of at most 0.0042.
Values sent between devices are 32-bit elements; how exact they have to be, the bound alone decides.
A program may use at most 128 MiB of HBM per device.

v0:
```python
import jax
import jax.numpy as jnp
from jax import lax
from jax.sharding import PartitionSpec as P

HEAD_COUNT = 128
HEAD_DIM = 64
STATE = 128
GROUPS = 8


def spread_2(block, axis, holder):
    block = jnp.where(lax.axis_index(axis) == holder, block, jnp.zeros_like(block))
    return lax.psum(block, axis)


def lookup(small_table, wanted):
    matches = wanted[:, None] == jnp.arange(small_table.shape[0], dtype=jnp.int32)[None, :]
    return jnp.sum(jnp.where(matches, small_table[None, :], 0), axis=1)


def on_device(
    head_values,
    gate_values,
    state_inputs,
    state_readout,
    log_decays,
    skip_gains,
    norm_gains,
    cached_states,
    owner_slots,
    prefix_blocks,
    prompt_sessions,
):
    prompts, block_len, feature_width = head_values.shape
    heads_here = feature_width // HEAD_DIM
    per_group = HEAD_COUNT // GROUPS
    local_groups = max(1, heads_here // per_group)
    group_heads = heads_here // local_groups
    seq_index = lax.axis_index("seq")
    cache_index = lax.axis_index("cache")
    first_group = cache_index * heads_here // per_group
    inputs_here = lax.dynamic_slice_in_dim(state_inputs, first_group, local_groups, 2)
    readout_here = lax.dynamic_slice_in_dim(state_readout, first_group, local_groups, 2)
    value_view = head_values.reshape(prompts, block_len, local_groups, group_heads, HEAD_DIM)
    decay_view = log_decays.reshape(prompts, block_len, local_groups, group_heads)
    positions = jnp.arange(block_len, dtype=jnp.int32)
    causal = positions[:, None] >= positions[None, :]
    intra_all, cumul_all, state_all, ending_all = ([], [], [], [])
    which_prompt = 0
    intra_list = []
    cumul_list = []
    state_list = []
    ending_list = []
    for which_group in range(local_groups):
        cumulative = jnp.cumsum(decay_view[which_prompt, :, which_group], axis=0)
        input_rows = inputs_here[which_prompt, :, which_group]
        readout_rows = readout_here[which_prompt, :, which_group]
        value_rows = value_view[which_prompt, :, which_group]
        scores = jnp.dot(readout_rows, input_rows.T, preferred_element_type=jnp.float32)

        def one_head(operands):
            cumul_head, value_head = operands
            spread = jnp.exp(jnp.where(causal, cumul_head[:, None] - cumul_head[None, :], -jnp.inf))
            mixing = (scores * spread).astype(jnp.bfloat16)
            return jnp.dot(mixing, value_head, preferred_element_type=jnp.float32)

        intra_term = lax.map(one_head, (cumulative.T, jnp.moveaxis(value_rows, 1, 0)))
        tail_decay = jnp.exp(cumulative[-1][None, :] - cumulative)
        scaled = (value_rows.astype(jnp.float32) * tail_decay[:, :, None]).astype(jnp.bfloat16)
        local_state = jnp.einsum(
            "shp,sn->hpn", scaled, input_rows, preferred_element_type=jnp.float32
        )
        intra_list.append(jnp.moveaxis(intra_term, 0, 1))
        cumul_list.append(cumulative)
        state_list.append(local_state)
        ending_list.append(jnp.exp(cumulative[-1]))
    intra_all.append(jnp.stack(intra_list, axis=1))
    cumul_all.append(jnp.stack(cumul_list, axis=1))
    state_all.append(jnp.concatenate(state_list, axis=0))
    ending_all.append(jnp.concatenate(ending_list, axis=0))
    intra_terms = jnp.stack(intra_all)
    cumulatives = jnp.stack(cumul_all)
    block_states = jnp.stack(state_all)
    block_decays = jnp.stack(ending_all)
    cached_len = lookup(prefix_blocks, prompt_sessions)
    slot_rows = lookup(owner_slots, prompt_sessions)
    owned = cached_states.shape[0]
    which_prompt = 0
    target = slot_rows[which_prompt]
    own_row = lax.dynamic_index_in_dim(cached_states, target % owned, 0, keepdims=False)
    received = [spread_2(own_row, "seq", target // owned)]
    fetched = jnp.stack(received)
    inject = seq_index == cached_len - 1
    block_decays = jnp.where(inject[:, None], 0.0, block_decays)
    block_states = jnp.where(inject[:, None, None, None], fetched, block_states)
    every_decay, every_state = (
        lax.all_gather(block_decays[None], "seq", axis=0, tiled=True),
        lax.all_gather(block_states[None], "seq", axis=0, tiled=True),
    )
    device_count = every_decay.shape[0]
    device_order = jnp.arange(device_count, dtype=jnp.int32)
    between = (device_order[None, :] > device_order[:, None]) & (device_order[None, :] < seq_index)
    factor = jnp.prod(jnp.where(between[:, :, None, None], every_decay[None, :, :, :], 1.0), axis=1)
    factor = jnp.where((device_order < seq_index)[:, None, None], factor, 0.0)
    incoming = jnp.einsum("jrh,jrhpn->rhpn", factor, every_state, precision=lax.Precision.HIGHEST)
    incoming_view = incoming.reshape(prompts, local_groups, group_heads, HEAD_DIM, STATE)
    carried = jnp.einsum(
        "rtgn,rghpn->rtghp",
        readout_here.astype(jnp.float32),
        incoming_view,
        precision=lax.Precision.HIGHEST,
    )
    carried = carried * jnp.exp(cumulatives)[..., None]
    skip_term = skip_gains.reshape(local_groups, group_heads)[
        None, None, :, :, None
    ] * value_view.astype(jnp.float32)
    summed = intra_terms + carried + skip_term
    live = (seq_index >= cached_len)[:, None, None, None, None]
    summed = jnp.where(live, summed, 0.0)
    gated = summed * jax.nn.silu(
        gate_values.reshape(prompts, block_len, local_groups, group_heads, HEAD_DIM).astype(
            jnp.float32
        )
    )
    mean_square = jnp.mean(gated * gated, axis=4, keepdims=True)
    normed = (
        gated
        * lax.rsqrt(mean_square + 1e-05)
        * norm_gains.reshape(local_groups, group_heads, HEAD_DIM)
    )
    return normed.reshape(prompts, block_len, feature_width).astype(jnp.bfloat16)


def solution(mesh):
    in_specs = (
        P("groups", "seq", ("head", "cache")),
        P("groups", "seq", ("head", "cache")),
        P("groups", "seq", "head", None),
        P("groups", "seq", "head", None),
        P("groups", "seq", ("head", "cache")),
        P(("head", "cache")),
        P(("head", "cache")),
        P(("groups", "seq"), ("head", "cache"), None, None),
        P("groups"),
        P("groups"),
        P("groups"),
    )
    out_specs = P("groups", "seq", ("head", "cache"))
    return jax.shard_map(
        on_device, mesh=mesh, in_specs=in_specs, out_specs=out_specs, check_vma=False
    )
```

profile of v0, /device:TPU:0, one launch (start us, length us, event | category | flops | bytes accessed | tf_op | source)
XLA Modules:
  0.0 252.4 jit_solution(4079366371963712770)
XLA Ops:
  14.7 4.5 %reduce-window.14 = f32[16,8,128]{2,1,0:T(8,128)S(1)} reduce-window(f32[16,8,128]{2,1,0:T(8,128)S(1)} %bitcast.178, f32[]{:T(128)} %constant.83.clone.1), window={size=1x1x128 pad=0_0x0_0x127_0}, to_apply=%region_1.2 | reduce-window | flops 2080768 | bytes 131076 | tf_op jit(solution)/shard_map/reduce-window
  19.7 4.5 %reduce-window.16 = f32[16,8,128]{2,1,0:T(8,128)S(1)} reduce-window(f32[16,8,128]{2,1,0:T(8,128)S(1)} %bitcast.179, f32[]{:T(128)} %constant.83.clone.1), window={size=1x1x128 pad=0_0x0_0x127_0}, to_apply=%region_5.6 | reduce-window | flops 2080768 | bytes 131076 | tf_op jit(solution)/shard_map/reduce-window.2
  25.9 6.4 %copy.49 = bf16[1,1024,2048]{1,2,0:T(8,128)(2,1)} copy(bf16[1,1024,2048]{2,1,0:T(8,128)(2,1)} %param.15) | data formatting | bytes 8388608 | tf_op args[0]
  32.3 5.2 %slice_bitcast_fusion.1 = (bf16[16,1024,64]{1,2,0:T(8,128)(2,1)}, bf16[16,1024,64]{1,2,0:T(8,128)(2,1)}) fusion(bf16[1,1024,2,16,64]{1,4,3,2,0:T(8,128)(2,1)} %bitcast.164), kind=kLoop, calls=%fused_computation.43 | loop fusion | bytes 8388608 | tf_op jit(solution)/shard_map/transpose | solution.py:68
  43.7 61.4 %while.22 = (s32[]{:T(128)}, f32[16,1024,64]{1,2,0:T(8,128)}, f32[16,1024]{1,0:T(8,128)S(1)}, f32[1024,1024]{1,0:T(8,128)}, bf16[16,1024,64]{1,2,0:T(8,128)(2,1)}, /*index=5*/s32[]{:T(128)}) while((s32[]{:T(128)}, f32[16,1024,64]{1,2,0:T(8,128)}, f32[16,1024]{1,0:T(8,128)S(1)}, f32[1024,1024]{1,0:T(8,128)}, ...), condition=%wide.region_4.5_spmd.clone, body=%wide.region_3.4_spmd.clone.sunk | while | flops 139460608 | bytes 4605001 | solution.py:68
  47.5 3.9 %fusion.60 = f32[16,1024,64]{1,2,0:T(8,128)} fusion(f32[16,1024,64]{1,2,0:T(8,128)} %get-tuple-element.261, s32[]{:T(128)} %get-tuple-element.260, f32[1024,1024]{1,0:T(8,128)} %get-tuple-element.269, f32[1024]{0:T(1024)S(1)} %bitcast.181, bf16[16,1024,64]{1,2,0:T(8,128)(2,1)} %get-tuple-element.270), kind=kOutput, calls=%fused_computation.6.clone.1 | convolution fusion | flops 139460608 | bytes 4596736 | tf_op jit(solution)/shard_map/while/body/eval_jaxpr/dot_general | solution.py:66
  51.5 3.8 %fusion.60 = f32[16,1024,64]{1,2,0:T(8,128)} fusion(f32[16,1024,64]{1,2,0:T(8,128)} %get-tuple-element.261, s32[]{:T(128)} %get-tuple-element.260, f32[1024,1024]{1,0:T(8,128)} %get-tuple-element.269, f32[1024]{0:T(1024)S(1)} %bitcast.181, bf16[16,1024,64]{1,2,0:T(8,128)(2,1)} %get-tuple-element.270), kind=kOutput, calls=%fused_computation.6.clone.1 | convolution fusion | flops 139460608 | bytes 4596736 | tf_op jit(solution)/shard_map/while/body/eval_jaxpr/dot_general | solution.py:66
  55.3 3.9 %fusion.60 = f32[16,1024,64]{1,2,0:T(8,128)} fusion(f32[16,1024,64]{1,2,0:T(8,128)} %get-tuple-element.261, s32[]{:T(128)} %get-tuple-element.260, f32[1024,1024]{1,0:T(8,128)} %get-tuple-element.269, f32[1024]{0:T(1024)S(1)} %bitcast.181, bf16[16,1024,64]{1,2,0:T(8,128)(2,1)} %get-tuple-element.270), kind=kOutput, calls=%fused_computation.6.clone.1 | convolution fusion | flops 139460608 | bytes 4596736 | tf_op jit(solution)/shard_map/while/body/eval_jaxpr/dot_general | solution.py:66
  59.2 3.8 %fusion.60 = f32[16,1024,64]{1,2,0:T(8,128)} fusion(f32[16,1024,64]{1,2,0:T(8,128)} %get-tuple-element.261, s32[]{:T(128)} %get-tuple-element.260, f32[1024,1024]{1,0:T(8,128)} %get-tuple-element.269, f32[1024]{0:T(1024)S(1)} %bitcast.181, bf16[16,1024,64]{1,2,0:T(8,128)(2,1)} %get-tuple-element.270), kind=kOutput, calls=%fused_computation.6.clone.1 | convolution fusion | flops 139460608 | bytes 4596736 | tf_op jit(solution)/shard_map/while/body/eval_jaxpr/dot_general | solution.py:66
  106.3 12.7 %all_gather.6 = f32[4,1,32]{2,1,0:T(1,128)S(1)} all-gather(f32[1,1,32]{2,1,0:T(1,128)S(1)} %broadcast_select_fusion), channel_id=1, replica_groups=mesh['groups'=2,'seq'=4,'head'=2,'cache'=2] {'seq'}, dimensions={0}, use_global_device_ids=true | all-gather | bytes 640 | tf_op jit(solution)/shard_map/all_gather | solution.py:98
  119.3 6.9 %copy.54 = f32[1,1024,2048]{1,2,0:T(8,128)} copy(bf16[1,1024,2048]{2,1,0:T(8,128)(2,1)} %param.16) | data formatting | bytes 12582912 | tf_op jit(solution)/shard_map/convert_element_type | solution.py:122
  136.1 61.8 %while.23 = (s32[]{:T(128)}, f32[16,1024,64]{1,2,0:T(8,128)}, f32[16,1024]{1,0:T(8,128)S(1)}, f32[1024,1024]{1,0:T(8,128)}, bf16[16,1024,64]{1,2,0:T(8,128)(2,1)}, /*index=5*/s32[]{:T(128)}) while((s32[]{:T(128)}, f32[16,1024,64]{1,2,0:T(8,128)}, f32[16,1024]{1,0:T(8,128)S(1)}, f32[1024,1024]{1,0:T(8,128)}, ...), condition=%wide.region_8.9_spmd.clone, body=%wide.region_7.8_spmd.clone.sunk | while | flops 139460608 | bytes 4605001 | solution.py:68
  140.0 4.1 %fusion.62 = f32[16,1024,64]{1,2,0:T(8,128)} fusion(f32[16,1024,64]{1,2,0:T(8,128)} %get-tuple-element.243, s32[]{:T(128)} %get-tuple-element.242, f32[1024,1024]{1,0:T(8,128)} %get-tuple-element.251, f32[1024]{0:T(1024)S(1)} %bitcast.182, bf16[16,1024,64]{1,2,0:T(8,128)(2,1)} %get-tuple-element.252), kind=kOutput, calls=%fused_computation.16.clone.1 | convolution fusion | flops 139460608 | bytes 4596736 | tf_op jit(solution)/shard_map/while/body/eval_jaxpr/dot_general | solution.py:66
  147.9 3.8 %fusion.62 = f32[16,1024,64]{1,2,0:T(8,128)} fusion(f32[16,1024,64]{1,2,0:T(8,128)} %get-tuple-element.243, s32[]{:T(128)} %get-tuple-element.242, f32[1024,1024]{1,0:T(8,128)} %get-tuple-element.251, f32[1024]{0:T(1024)S(1)} %bitcast.182, bf16[16,1024,64]{1,2,0:T(8,128)(2,1)} %get-tuple-element.252), kind=kOutput, calls=%fused_computation.16.clone.1 | convolution fusion | flops 139460608 | bytes 4596736 | tf_op jit(solution)/shard_map/while/body/eval_jaxpr/dot_general | solution.py:66
  151.7 3.9 %fusion.62 = f32[16,1024,64]{1,2,0:T(8,128)} fusion(f32[16,1024,64]{1,2,0:T(8,128)} %get-tuple-element.243, s32[]{:T(128)} %get-tuple-element.242, f32[1024,1024]{1,0:T(8,128)} %get-tuple-element.251, f32[1024]{0:T(1024)S(1)} %bitcast.182, bf16[16,1024,64]{1,2,0:T(8,128)(2,1)} %get-tuple-element.252), kind=kOutput, calls=%fused_computation.16.clone.1 | convolution fusion | flops 139460608 | bytes 4596736 | tf_op jit(solution)/shard_map/while/body/eval_jaxpr/dot_general | solution.py:66
  159.5 3.8 %fusion.62 = f32[16,1024,64]{1,2,0:T(8,128)} fusion(f32[16,1024,64]{1,2,0:T(8,128)} %get-tuple-element.243, s32[]{:T(128)} %get-tuple-element.242, f32[1024,1024]{1,0:T(8,128)} %get-tuple-element.251, f32[1024]{0:T(1024)S(1)} %bitcast.182, bf16[16,1024,64]{1,2,0:T(8,128)(2,1)} %get-tuple-element.252), kind=kOutput, calls=%fused_computation.16.clone.1 | convolution fusion | flops 139460608 | bytes 4596736 | tf_op jit(solution)/shard_map/while/body/eval_jaxpr/dot_general | solution.py:66
  163.3 3.9 %fusion.62 = f32[16,1024,64]{1,2,0:T(8,128)} fusion(f32[16,1024,64]{1,2,0:T(8,128)} %get-tuple-element.243, s32[]{:T(128)} %get-tuple-element.242, f32[1024,1024]{1,0:T(8,128)} %get-tuple-element.251, f32[1024]{0:T(1024)S(1)} %bitcast.182, bf16[16,1024,64]{1,2,0:T(8,128)(2,1)} %get-tuple-element.252), kind=kOutput, calls=%fused_computation.16.clone.1 | convolution fusion | flops 139460608 | bytes 4596736 | tf_op jit(solution)/shard_map/while/body/eval_jaxpr/dot_general | solution.py:66
  174.9 3.9 %fusion.62 = f32[16,1024,64]{1,2,0:T(8,128)} fusion(f32[16,1024,64]{1,2,0:T(8,128)} %get-tuple-element.243, s32[]{:T(128)} %get-tuple-element.242, f32[1024,1024]{1,0:T(8,128)} %get-tuple-element.251, f32[1024]{0:T(1024)S(1)} %bitcast.182, bf16[16,1024,64]{1,2,0:T(8,128)(2,1)} %get-tuple-element.252), kind=kOutput, calls=%fused_computation.16.clone.1 | convolution fusion | flops 139460608 | bytes 4596736 | tf_op jit(solution)/shard_map/while/body/eval_jaxpr/dot_general | solution.py:66
  178.7 3.8 %fusion.62 = f32[16,1024,64]{1,2,0:T(8,128)} fusion(f32[16,1024,64]{1,2,0:T(8,128)} %get-tuple-element.243, s32[]{:T(128)} %get-tuple-element.242, f32[1024,1024]{1,0:T(8,128)} %get-tuple-element.251, f32[1024]{0:T(1024)S(1)} %bitcast.182, bf16[16,1024,64]{1,2,0:T(8,128)(2,1)} %get-tuple-element.252), kind=kOutput, calls=%fused_computation.16.clone.1 | convolution fusion | flops 139460608 | bytes 4596736 | tf_op jit(solution)/shard_map/while/body/eval_jaxpr/dot_general | solution.py:66
  186.4 3.9 %fusion.62 = f32[16,1024,64]{1,2,0:T(8,128)} fusion(f32[16,1024,64]{1,2,0:T(8,128)} %get-tuple-element.243, s32[]{:T(128)} %get-tuple-element.242, f32[1024,1024]{1,0:T(8,128)} %get-tuple-element.251, f32[1024]{0:T(1024)S(1)} %bitcast.182, bf16[16,1024,64]{1,2,0:T(8,128)(2,1)} %get-tuple-element.252), kind=kOutput, calls=%fused_computation.16.clone.1 | convolution fusion | flops 139460608 | bytes 4596736 | tf_op jit(solution)/shard_map/while/body/eval_jaxpr/dot_general | solution.py:66
  198.0 15.2 %all-gather.3.cloned.1.call-done = f32[128,64,128]{2,1,0:T(8,128)} async-done(((f32[32,64,128]{2,1,0:T(8,128)}), f32[128,64,128]{2,1,0:T(8,128)}) %all-gather.3.cloned.1.call-update) | async-done | bytes 4194320 | tf_op jit(solution)/shard_map/all_gather | solution.py:99
  213.1 12.7 %fusion.22 = f32[32,1,64,128]{3,1,2,0:T(1,128)S(1)} fusion(f32[4,32,1,1]{0,2,3,1:T(1,128)S(1)} %copy.56, f32[4,32,64,128]{3,2,1,0:T(8,128)} %bitcast.170), kind=kOutput, calls=%fused_computation.30 | convolution fusion | flops 12582912 | bytes 5243392 | tf_op jit(solution)/shard_map/jrh,jrhpn->rhpn/dot_general | solution.py:106
  225.8 10.7 %multiply_reduce_fusion = (f32[1024,2,16]{0,2,1:T(8,128)S(1)}, f32[1,1024,2,16,64]{1,4,3,2,0:T(8,128)S(1)}) fusion(f32[1,1024,2,16,64]{1,4,3,2,0:T(8,128)} %bitcast.169, bf16[1,1024,2,16,64]{1,4,3,2,0:T(8,128)(2,1)S(1)} %bitcast.167, f32[2,16]{1,0:T(2,128)S(1)} %mul.96, f32[1024,2,16]{0,2,1:T(8,128)S(1)} %maximum_exponential_fusion, ...), kind=kOutput, calls=%fused_computation.29 | convolution fusion | flops 3250552832 | bytes 31195264 | tf_op jit(solution)/shard_map/rtgn,rghpn->rtghp/dot_general | solution.py:108
  239.1 6.5 %copy.55 = bf16[1,1024,2048]{2,1,0:T(8,128)(2,1)} copy(bf16[1,1024,2048]{1,2,0:T(8,128)(2,1)} %bitcast.168) | data formatting | bytes 8388608 | tf_op jit(solution)/shard_map/convert_element_type | solution.py:132
  (116 shorter events, 102.4 us)
Async XLA Ops:
  6.5 18.7 %copy-start = (bf16[1,1024,4,128]{3,2,1,0:T(4,128)(2,1)S(1)}, bf16[1,1024,4,128]{3,2,1,0:T(4,128)(2,1)}, u32[]{:S(2)}) copy-start(bf16[1,1024,4,128]{3,2,1,0:T(4,128)(2,1)} %param.18) | copy-start | bytes 3145732
  6.5 126.0 %all-reduce.2.cloned.1.call-start = ((), (), s32[]{:S(2)}) async-start(), calls=%async_computation | async-start | bytes 2097152 | tf_op jit(solution)/shard_map/psum | solution.py:14
  13.7 199.4 %all-gather.3.cloned.1.call-start = ((), (), s32[]{:S(2)}) async-start(), calls=%async_computation.1 | async-start | bytes 5242880 | tf_op jit(solution)/shard_map/all_gather | solution.py:99
  32.3 5.2 %copy-start.4 = (bf16[1,1024,4,128]{3,2,1,0:T(4,128)(2,1)S(1)}, bf16[1,1024,4,128]{3,2,1,0:T(4,128)(2,1)}, u32[]{:S(2)}) copy-start(bf16[1,1024,4,128]{3,2,1,0:T(4,128)(2,1)} %param.17) | copy-start | bytes 3145732
  119.3 6.9 %copy-start.6 = (f32[32]{0:T(128)S(1)}, f32[32]{0:T(128)}, u32[]{:S(2)}) copy-start(f32[32]{0:T(128)} %param.20) | copy-start | bytes 388
  119.3 7.0 %copy-start.5 = (f32[2048]{0:T(1024)S(1)}, f32[2048]{0:T(1024)}, u32[]{:S(2)}) copy-start(f32[2048]{0:T(1024)} %param.21) | copy-start | bytes 24580
  126.3 2.8 %copy-start.2 = (bf16[1,1024,2048]{1,2,0:T(8,128)(2,1)S(1)}, bf16[1,1024,2048]{1,2,0:T(8,128)(2,1)}, u32[]{:S(2)}) copy-start(bf16[1,1024,2048]{1,2,0:T(8,128)(2,1)} %copy.49) | copy-start | bytes 12582916
  213.1 12.7 %copy-start.3 = (bf16[1,1024,2048]{1,2,0:T(8,128)(2,1)S(1)}, bf16[1,1024,2048]{1,2,0:T(8,128)(2,1)}, u32[]{:S(2)}) copy-start(bf16[1,1024,2048]{1,2,0:T(8,128)(2,1)} %copy.49) | copy-start | bytes 12582916
  239.1 6.5 %copy-start.1 = (bf16[1,1024,4,128]{3,2,1,0:T(4,128)(2,1)S(1)}, bf16[1,1024,4,128]{3,2,1,0:T(4,128)(2,1)}, u32[]{:S(2)}) copy-start(bf16[1,1024,4,128]{3,2,1,0:T(4,128)(2,1)} %param.18) | copy-start | bytes 3145732
Sparse Core Ops, SparseCore 0:
  13.8 54.3 all-reduce.1
  133.8 79.2 all-gather.2
where the time goes:
time: 254 us; the launch traced here: 252 us
  matrix products  155 us (61%)
  local copies, waits for them, and re-layouts  34.4 us (14%)
  between operations  18.2 us (7%)
  other arithmetic  17.1 us (7%)
  waiting for transfers between devices  15.2 us (6%)
  blocking collectives  12.7 us (5%)
    dot_general x32, matrix products, one_head(): return jnp.dot(mixing, value_head, preferred_element_type=jnp.float32)  123 us
    all_gather x1, waiting for transfers between devices, on_device(): lax.all_gather(block_states[None], 'seq', axis=0, tiled=True)  15.2 us
    dot_general x1, matrix products, on_device(): jnp.einsum('jrh,jrhpn->rhpn', factor, every_state, precision=lax.Precisio...  12.7 us
    all_gather x1, blocking collectives, on_device(): lax.all_gather(block_decays[None], 'seq', axis=0, tiled=True)  12.7 us
    dot_general x1, matrix products, on_device(): jnp.einsum('rtgn,rghpn->rtghp', readout_here.astype(jnp.float32), incomin...  10.7 us
    another operation x6, other arithmetic  9.27 us
    unnamed x19, local copies, waits for them, and re-layouts  7.74 us
    convert_element_type x1, local copies, waits for them, and re-layouts, on_device(): gate_values.reshape(prompts, block_len, local_groups, group_heads, HEAD_DIM)  6.89 us
  transfers between devices with their start and end apart: 2, of which 1 were waited for; matrix products, arithmetic and copies ran while one was open for 67% of the time, Pallas kernels for 0%

commit v1 on v0

v1 whole, which is shorter than its diff:
```python
import functools

import jax
import jax.numpy as jnp
from jax import lax
from jax.experimental import pallas as pl
from jax.experimental.pallas import tpu as pltpu
from jax.sharding import PartitionSpec as P

HEAD_COUNT = 128
HEAD_DIM = 64
STATE = 128
GROUPS = 8
SUB = 128
PAIR = 2 * HEAD_DIM
LOG2E = 1.4426950408889634
F32 = jnp.float32
BF16 = jnp.bfloat16
MESH = pl.DeviceIdType.MESH


def split_rows(x):
    high = x.astype(BF16)
    low = (x - high.astype(F32)).astype(BF16)
    return jnp.concatenate([high, low], axis=0)


def kernel(
    n_seq, pairs, pairs_per_group, subs, owned_rows,
    sessions_ref, slots_ref, prefix_ref, skip_ref,
    inputs_ref, readout_ref, decays_ref, norm_ref, cached_ref, values_hbm, gates_hbm,
    out_hbm,
    vbuf, gbuf, obuf, acc, dec, own, bsend, brecv, fsend, frecv, local, ending,
    cum3, cum_t, cum_pad, scores, inputs_t, readout2,
    vsem, gsem, osem, bsend_sem, brecv_sem, fsend_sem, frecv_sem,
):
    me = lax.axis_index("seq")
    heads = 2 * pairs
    groups = pairs // pairs_per_group
    last = n_seq - 1

    def value_copy(c):
        return pltpu.make_async_copy(
            values_hbm.at[0, :, pl.ds(pl.multiple_of(c * PAIR, PAIR), PAIR)], vbuf.at[c], vsem.at[c]
        )

    def gate_copy(c):
        return pltpu.make_async_copy(
            gates_hbm.at[0, :, pl.ds(pl.multiple_of(c * PAIR, PAIR), PAIR)], gbuf.at[c], gsem.at[c]
        )

    def out_copy(c):
        return pltpu.make_async_copy(
            obuf.at[c], out_hbm.at[0, :, pl.ds(pl.multiple_of(c * PAIR, PAIR), PAIR)], osem.at[c]
        )

    def back_copy(src, c):
        return pltpu.make_async_remote_copy(
            src_ref=src.at[c], dst_ref=brecv.at[c], send_sem=bsend_sem.at[c],
            recv_sem=brecv_sem.at[c], device_id={"seq": me - 1}, device_id_type=MESH,
        )

    def forward_copy(src, c):
        return pltpu.make_async_remote_copy(
            src_ref=src.at[c], dst_ref=frecv.at[c], send_sem=fsend_sem.at[c],
            recv_sem=frecv_sem.at[c], device_id={"seq": me + 1}, device_id_type=MESH,
        )

    barrier = pltpu.get_barrier_semaphore()

    @pl.when(me > 0)
    def _():
        pl.semaphore_signal(barrier, inc=1, device_id={"seq": me - 1}, device_id_type=MESH)

    @pl.when(me < last)
    def _():
        pl.semaphore_signal(barrier, inc=1, device_id={"seq": me + 1}, device_id_type=MESH)

    @pl.loop(0, pairs)
    def _(c):
        value_copy(c).start()
        gate_copy(c).start()

    session = sessions_ref[0]
    slot = slots_ref[session]
    k = prefix_ref[session]
    owner = slot // owned_rows
    row_here = slot % owned_rows

    @pl.when((me > 0) & (me < last))
    def _():
        pl.semaphore_wait(barrier, 2)

    @pl.when((me == 0) | (me == last))
    def _():
        pl.semaphore_wait(barrier, 1)

    @pl.loop(0, pairs)
    def _(c):
        row = cached_ref[0, c]
        for other in range(1, owned_rows):
            row = jnp.where(row_here == other, cached_ref[other, c], row)
        row = row.T
        own[c] = row

        @pl.when(me == last)
        def _():
            bsend[c] = row
            back_copy(own, c).start()

        @pl.when(me == 0)
        def _():
            bsend[c] = row
            frecv[c] = row
            forward_copy(own, c).start()

    rows = lax.broadcasted_iota(jnp.int32, (SUB, SUB), 0)
    lanes = lax.broadcasted_iota(jnp.int32, (SUB, SUB), 1)
    causal = rows >= lanes
    tri = jnp.where(causal, 1.0, 0.0).astype(F32)
    for q in range(subs):
        at = pl.ds(q * SUB, SUB)
        cum = jnp.dot(
            tri, decays_ref[at, :] * LOG2E, precision=lax.Precision.HIGHEST,
            preferred_element_type=F32,
        )
        cum_pad[...] = jnp.zeros_like(cum_pad)
        cum_pad[:, :heads] = cum
        cum = cum_pad[...]
        cum_t[q] = cum.T
        high = cum.astype(BF16).astype(F32)
        middle = (cum - high).astype(BF16).astype(F32)
        low = (cum - high - middle).astype(BF16).astype(F32)
        cum3[at, :] = (
            high + pltpu.roll(middle, heads, axis=1) + pltpu.roll(low, 2 * heads, axis=1)
        ).astype(BF16)
        for g in range(groups):
            c_rows = readout_ref[g, at, :]
            b_rows = inputs_ref[g, at, :]
            product = lax.dot_general(
                c_rows, b_rows, (((1,), (1,)), ((), ())), preferred_element_type=F32
            )
            scores[g, q] = jnp.where(causal, product, 0.0)
            inputs_t[g, q] = b_rows.astype(F32).T.astype(BF16)
            readout2[g, at, :] = jnp.concatenate([c_rows, c_rows], axis=1)

    first_half = lanes < HEAD_DIM
    first_row = first_half[:1]
    spread_rows = lax.broadcasted_iota(jnp.int32, (128, 2 * SUB), 0)
    spread_lanes = lax.broadcasted_iota(jnp.int32, (128, 2 * SUB), 1)
    mean_of = jnp.where((rows < HEAD_DIM) == first_half, 1.0 / HEAD_DIM, 0.0).astype(BF16)

    def stage_one(c):
        g = c // pairs_per_group
        value_copy(c).wait()
        wanted = 2 * c + (spread_lanes >= SUB).astype(jnp.int32)
        pick = jnp.where(
            (spread_rows < 3 * heads) & ((spread_rows % heads) == wanted), 1.0, 0.0
        ).astype(BF16)
        skip_row = jnp.where(first_row, skip_ref[2 * c], skip_ref[2 * c + 1])
        state = None
        offset = jnp.zeros((1, PAIR), F32)
        for q in range(subs):
            at = pl.ds(q * SUB, SUB)
            cum = jnp.dot(cum3[at, :], pick, preferred_element_type=F32)
            cum0, cum1 = cum[:, :SUB], cum[:, SUB:]
            score = scores[g, q]
            mix0 = score * jnp.exp2(jnp.minimum(cum0 - cum_t[q, pl.ds(2 * c, 1), :], 0.0))
            mix1 = score * jnp.exp2(jnp.minimum(cum1 - cum_t[q, pl.ds(2 * c + 1, 1), :], 0.0))
            mix = jnp.concatenate([mix0.astype(BF16), mix1.astype(BF16)], axis=1)
            value = vbuf[c, at, :]
            value32 = value.astype(F32)
            zero = jnp.zeros_like(value32)
            both = jnp.concatenate(
                [
                    jnp.where(first_half, value32, zero).astype(BF16),
                    jnp.where(first_half, zero, value32).astype(BF16),
                ],
                axis=0,
            )
            total = jnp.dot(mix, both, preferred_element_type=F32) + skip_row * value32
            cum_p = jnp.where(first_half, cum0, cum1)
            end = cum_p[SUB - 1 :, :]
            decay = jnp.exp2(cum_p)
            if state is not None:
                total += decay * jnp.dot(
                    readout2[g, at, :], split_rows(state), preferred_element_type=F32
                )
            acc[c, at, :] = total
            dec[c, at, :] = decay * jnp.exp2(offset)
            scaled = (value32 * jnp.exp2(end - cum_p)).astype(BF16)
            here = jnp.dot(inputs_t[g, q], scaled, preferred_element_type=F32)
            state = here if state is None else jnp.exp2(end) * state + here
            offset = offset + end
        local[c] = state
        ending[c] = jnp.broadcast_to(jnp.exp2(offset), (8, PAIR))

    def back_step(c):
        back_copy(own, c).wait_recv()
        bsend[c] = jnp.where(owner == me, own[c], brecv[c])

        @pl.when(me >= 2)
        def _():
            back_copy(bsend, c).start()

    def finish(c):
        g = c // pairs_per_group

        @pl.when(me > 0)
        def _():
            forward_copy(own, c).wait_recv()

        below = frecv[c]
        cached = jnp.where(owner == me, own[c], jnp.where(owner > me, bsend[c], below))
        carry = jnp.where(me == k, cached, below)

        @pl.when((me > 0) & (me < last))
        def _():
            onward = ending[c, :1, :] * carry + local[c]
            fsend[c] = jnp.where(me < k, cached, onward)
            forward_copy(fsend, c).start()

        gate_copy(c).wait()
        carry2 = split_rows(carry)
        norm_row = norm_ref[pl.ds(c, 1), :]
        live = me >= k
        for q in range(subs):
            at = pl.ds(q * SUB, SUB)
            carried = jnp.dot(readout2[g, at, :], carry2, preferred_element_type=F32)
            summed = acc[c, at, :] + dec[c, at, :] * carried
            summed = jnp.where(live, summed, 0.0)
            gate = gbuf[c, at, :].astype(F32)
            half = 0.5 * gate
            gated = summed * (half + half * jnp.tanh(half))
            mean = jnp.dot((gated * gated).astype(BF16), mean_of, preferred_element_type=F32)
            obuf[c, at, :] = (gated * lax.rsqrt(mean + 1e-5) * norm_row).astype(BF16)
        out_copy(c).start()

    relays = (me > 0) & (me < last)
    ahead = jnp.where((me >= 2) & (me < last), jnp.minimum(pairs, 5 * (me - 1)), 0)

    @pl.loop(0, pairs + ahead)
    def _(step):
        @pl.when(step < pairs)
        def _():
            @pl.when(relays & (me >= 2))
            def _():
                back_step(step)

            stage_one(step)

            @pl.when(relays & (me < 2))
            def _():
                back_step(step)

        @pl.when(step >= ahead)
        def _():
            finish(step - ahead)

    @pl.loop(0, pairs)
    def _(c):
        out_copy(c).wait()

        @pl.when(me >= 2)
        def _():
            back_copy(own, c).wait_send()

        @pl.when(me < last)
        def _():
            forward_copy(own, c).wait_send()


def on_device(
    n_seq,
    head_values,
    gate_values,
    state_inputs,
    state_readout,
    log_decays,
    skip_gains,
    norm_gains,
    cached_states,
    owner_slots,
    prefix_blocks,
    prompt_sessions,
):
    _, block, width = head_values.shape
    heads = width // HEAD_DIM
    per_group = HEAD_COUNT // GROUPS
    groups = max(1, heads // per_group)
    pairs = heads // 2
    subs = block // SUB
    owned = cached_states.shape[0]
    first = lax.axis_index("cache") * heads // per_group
    inputs = jnp.moveaxis(lax.dynamic_slice_in_dim(state_inputs, first, groups, 2)[0], 1, 0)
    readout = jnp.moveaxis(lax.dynamic_slice_in_dim(state_readout, first, groups, 2)[0], 1, 0)
    smem = pl.BlockSpec(memory_space=pltpu.SMEM)
    vmem = pl.BlockSpec(memory_space=pltpu.VMEM)
    hbm = pl.BlockSpec(memory_space=pl.ANY)
    tiles = pltpu.VMEM((pairs, STATE, PAIR), F32)
    sems = pltpu.SemaphoreType.DMA((pairs,))
    return pl.pallas_call(
        functools.partial(kernel, n_seq, pairs, pairs // groups, subs, owned),
        out_shape=jax.ShapeDtypeStruct(head_values.shape, BF16),
        in_specs=[smem] * 4 + [vmem] * 5 + [hbm] * 2,
        out_specs=hbm,
        scratch_shapes=[
            pltpu.VMEM((pairs, block, PAIR), BF16),
            pltpu.VMEM((pairs, block, PAIR), BF16),
            pltpu.VMEM((pairs, block, PAIR), BF16),
            pltpu.VMEM((pairs, block, PAIR), F32),
            pltpu.VMEM((pairs, block, PAIR), F32),
            tiles, tiles, tiles, tiles, tiles, tiles,
            pltpu.VMEM((pairs, 8, PAIR), F32),
            pltpu.VMEM((block, 128), BF16),
            pltpu.VMEM((subs, 128, SUB), F32),
            pltpu.VMEM((SUB, 128), F32),
            pltpu.VMEM((groups, subs, SUB, SUB), F32),
            pltpu.VMEM((groups, subs, STATE, SUB), BF16),
            pltpu.VMEM((groups, block, 2 * STATE), BF16),
            sems, sems, sems, sems, sems, sems, sems,
        ],
        compiler_params=pltpu.CompilerParams(
            collective_id=0, has_side_effects=True, vmem_limit_bytes=58 * 1024 * 1024
        ),
        name="scan_chain",
    )(
        prompt_sessions, owner_slots, prefix_blocks, skip_gains,
        inputs, readout, log_decays[0], norm_gains.reshape(pairs, PAIR),
        cached_states.reshape(owned, pairs, PAIR, STATE), head_values, gate_values,
    )


def solution(mesh):
    in_specs = (
        P("groups", "seq", ("head", "cache")),
        P("groups", "seq", ("head", "cache")),
        P("groups", "seq", "head", None),
        P("groups", "seq", "head", None),
        P("groups", "seq", ("head", "cache")),
        P(("head", "cache")),
        P(("head", "cache")),
        P(("groups", "seq"), ("head", "cache"), None, None),
        P("groups"),
        P("groups"),
        P("groups"),
    )
    return jax.shard_map(
        functools.partial(on_device, mesh.shape["seq"]), mesh=mesh, in_specs=in_specs,
        out_specs=P("groups", "seq", ("head", "cache")), check_vma=False,
    )
```

time: 254 us -> 83.7 us (0.33)
  the two profiles are of different devices: /device:TPU:0 before, /device:TPU:24 now
where the time goes in v1:
time: 83.7 us; the launch traced here: 83.5 us
  Pallas kernels  71.8 us (86%)
  local copies, waits for them, and re-layouts  11.1 us (13%)
    pallas_call x1, Pallas kernels, on_device(): pl.pallas_call(functools.partial(kernel, n_seq, pairs, pairs // groups, s...  71.8 us
    unnamed x2, local copies, waits for them, and re-layouts  6.71 us
    dynamic_slice x2, local copies, waits for them, and re-layouts, on_device(): lax.dynamic_slice_in_dim(state_readout, first, groups, 2)[0]  3.48 us

profile of v1, /device:TPU:24, one launch (start us, length us, event | category | flops | bytes accessed | tf_op | source)
XLA Modules:
  0.0 83.5 jit_solution(15919924803354519086)
XLA Ops:
  0.7 1.9 %copy.14 = f32[1,1024,32]{2,1,0:T(8,128)} copy(f32[1,1024,32]{1,2,0:T(8,128)} %param.15) | data formatting | bytes 262144 | tf_op args[4]
  2.6 2.6 %constant_dynamic-slice_fusion = (bf16[1,1024,2,128]{3,2,1,0:T(2,128)(2,1)S(1)}, bf16[1,1024,2,128]{3,2,1,0:T(2,128)(2,1)S(1)}) fusion(bf16[1,1024,4,128]{3,2,1,0:T(4,128)(2,1)} %param.14, s32[]{:T(128)S(6)} %select_n.10, bf16[1,1024,4,128]{3,2,1,0:T(4,128)(2,1)} %param.13), kind=kLoop, calls=%fused_computation.2 | loop fusion | bytes 2097156 | tf_op jit(solution)/shard_map/dynamic_slice | solution.py:296
  5.2 0.9 %copy.17 = bf16[1,1024,2,128]{3,1,2,0:T(8,128)(2,1)} copy(bf16[1,1024,2,128]{3,2,1,0:T(2,128)(2,1)S(1)} %get-tuple-element.5) | data formatting | bytes 1048576 | tf_op jit(solution)/shard_map/dynamic_slice | solution.py:296
  6.1 0.9 %copy.18 = bf16[1,1024,2,128]{3,1,2,0:T(8,128)(2,1)} copy(bf16[1,1024,2,128]{3,2,1,0:T(2,128)(2,1)S(1)} %get-tuple-element.6) | data formatting | bytes 1048576 | tf_op jit(solution)/shard_map/dynamic_slice | solution.py:295
  6.9 71.8 %scan_chain.1 = bf16[1,1024,2048]{2,1,0:T(8,128)(2,1)} custom-call(s32[1]{0:T(128)S(6)} %copy.20.sessions_ref, s32[8]{0:T(128)} %slots_ref.1, s32[8]{0:T(128)} %prefix_ref.1, f32[32]{0:T(128)} %skip_ref.1, bf16[2,1024,128]{2,1,0:T(8,128)(2,1)} %bitcast.15, bf16[2,1024,128]{2,1,0:T(8,128)(2,1)} %bitcast.14, f32[1024,32]{1,0:T(8,128)} %bitcast.13, ...), custom_call_target="tpu_custom_call" | custom-call | tf_op jit(solution)/shard_map/scan_chain/pallas_call | solution.py:302
  78.7 4.8 %copy.21 = bf16[1,1024,2048]{2,1,0:T(8,128)(2,1)} copy(bf16[1,1024,2048]{2,1,0:T(8,128)(2,1)} %scan_chain.1) | data formatting | bytes 8388608

commit v2 on v1

v2 whole, which is shorter than its diff:
```python
import functools

import jax
import jax.numpy as jnp
from jax import lax
from jax.experimental import pallas as pl
from jax.experimental.pallas import tpu as pltpu
from jax.sharding import PartitionSpec as P

HEAD_COUNT = 128
HEAD_DIM = 64
STATE = 128
GROUPS = 8
SUB = 128
PAIR = 2 * HEAD_DIM
LOG2E = 1.4426950408889634
QUAD = 2 * PAIR
F32 = jnp.float32
BF16 = jnp.bfloat16
MESH = pl.DeviceIdType.MESH


def split_rows(x):
    high = x.astype(BF16)
    low = (x - high.astype(F32)).astype(BF16)
    return jnp.concatenate([high, low], axis=0)


def kernel(
    n_seq, pairs, pairs_per_group, subs, owned_rows,
    sessions_ref, slots_ref, prefix_ref, skip_ref,
    *refs,
):
    me = lax.axis_index("seq")
    heads = 2 * pairs
    groups = pairs // pairs_per_group
    inputs_refs, readout_refs = refs[:groups], refs[groups : 2 * groups]
    (
        decays_ref, norm_ref, cached_ref, values_hbm, gates_hbm, out_hbm, live_ref,
        vbuf, gbuf, obuf, acc, dec, own, bsend, brecv, fsend, frecv, local, ending,
        cum3, cum_t, cum_pad, scores, inputs_t, readout2, spread, big, squares,
        vsem, gsem, osem, bsend_sem, brecv_sem, fsend_sem, frecv_sem,
    ) = refs[2 * groups :]
    last = n_seq - 1

    def value_copy(c):
        return pltpu.make_async_copy(
            values_hbm.at[0, :, pl.ds(pl.multiple_of(c * PAIR, PAIR), PAIR)], vbuf.at[c], vsem.at[c]
        )

    def gate_copy(c):
        return pltpu.make_async_copy(
            gates_hbm.at[0, :, pl.ds(pl.multiple_of(c * PAIR, PAIR), PAIR)], gbuf.at[c], gsem.at[c]
        )

    def out_copy(c):
        return pltpu.make_async_copy(
            obuf.at[c], out_hbm.at[0, :, pl.ds(pl.multiple_of(c * PAIR, PAIR), PAIR)], osem.at[c]
        )

    def back_copy(src, c):
        return pltpu.make_async_remote_copy(
            src_ref=src.at[c], dst_ref=brecv.at[c], send_sem=bsend_sem.at[c],
            recv_sem=brecv_sem.at[c], device_id={"seq": me - 1}, device_id_type=MESH,
        )

    def forward_copy(src, c):
        return pltpu.make_async_remote_copy(
            src_ref=src.at[c], dst_ref=frecv.at[c], send_sem=fsend_sem.at[c],
            recv_sem=frecv_sem.at[c], device_id={"seq": me + 1}, device_id_type=MESH,
        )

    barrier = pltpu.get_barrier_semaphore()

    @pl.when(me > 0)
    def _():
        pl.semaphore_signal(barrier, inc=1, device_id={"seq": me - 1}, device_id_type=MESH)

    @pl.when(me < last)
    def _():
        pl.semaphore_signal(barrier, inc=1, device_id={"seq": me + 1}, device_id_type=MESH)

    @pl.loop(0, pairs)
    def _(c):
        value_copy(c).start()
        gate_copy(c).start()

    session = sessions_ref[0]
    slot = slots_ref[session]
    k = prefix_ref[session]
    owner = slot // owned_rows
    row_here = slot % owned_rows
    live_ref[0] = (me >= k).astype(jnp.int32)

    @pl.when((me > 0) & (me < last))
    def _():
        pl.semaphore_wait(barrier, 2)

    @pl.when((me == 0) | (me == last))
    def _():
        pl.semaphore_wait(barrier, 1)

    @pl.loop(0, pairs)
    def _(c):
        row = cached_ref[0, c]
        for other in range(1, owned_rows):
            row = jnp.where(row_here == other, cached_ref[other, c], row)
        row = row.T
        own[c] = row

        @pl.when(me == last)
        def _():
            bsend[c] = row
            back_copy(own, c).start()

        @pl.when(me == 0)
        def _():
            bsend[c] = row
            frecv[c] = row
            forward_copy(own, c).start()

    rows = lax.broadcasted_iota(jnp.int32, (SUB, SUB), 0)
    lanes = lax.broadcasted_iota(jnp.int32, (SUB, SUB), 1)
    causal = rows >= lanes
    tri = jnp.where(rows <= lanes, 1.0, 0.0).astype(F32)
    cum_pad[...] = jnp.zeros_like(cum_pad)
    for q in range(subs):
        at = pl.ds(q * SUB, SUB)
        sums = jnp.dot(
            decays_ref[:, at] * LOG2E, tri, precision=lax.Precision.HIGHEST,
            preferred_element_type=F32,
        )
        cum_t[q] = sums
        cum_pad[:heads, :] = sums
        cum = cum_pad[...].T
        high = cum.astype(BF16).astype(F32)
        middle = (cum - high).astype(BF16).astype(F32)
        low = (cum - high - middle).astype(BF16).astype(F32)
        cum3[at, :] = (
            high + pltpu.roll(middle, heads, axis=1) + pltpu.roll(low, 2 * heads, axis=1)
        ).astype(BF16)
        for g in range(groups):
            c_rows = readout_refs[g][at, :]
            b_rows = inputs_refs[g][at, :]
            product = lax.dot_general(
                c_rows, b_rows, (((1,), (1,)), ((), ())), preferred_element_type=F32
            )
            scores[g, q] = jnp.where(causal, product, 0.0)
            inputs_t[g, q] = b_rows.astype(F32).T.astype(BF16)
            readout2[g, at, :] = jnp.concatenate([c_rows, c_rows], axis=1)

    wide_rows = lax.broadcasted_iota(jnp.int32, (QUAD, QUAD), 0)
    wide_lanes = lax.broadcasted_iota(jnp.int32, (QUAD, QUAD), 1)
    first_half = lanes < HEAD_DIM
    wide_half = (wide_lanes[:SUB] % PAIR) < HEAD_DIM
    row_half = wide_half[:1]
    spread_rows = lax.broadcasted_iota(jnp.int32, (128, 4 * SUB), 0)
    spread_lanes = lax.broadcasted_iota(jnp.int32, (128, 4 * SUB), 1)
    mean_of = jnp.where(
        wide_rows // HEAD_DIM == wide_lanes // HEAD_DIM, 1.0 / HEAD_DIM, 0.0
    ).astype(BF16)

    def stage_one(u):
        g = (2 * u) // pairs_per_group
        value_copy(2 * u).wait()
        value_copy(2 * u + 1).wait()
        wanted = 4 * u + spread_lanes // SUB
        pick = jnp.where(
            (spread_rows < 3 * heads) & ((spread_rows % heads) == wanted), 1.0, 0.0
        ).astype(BF16)
        spread[...] = jnp.dot(cum3[...], pick, preferred_element_type=F32)
        low_pair = jnp.where(row_half, skip_ref[4 * u], skip_ref[4 * u + 1])
        high_pair = jnp.where(row_half, skip_ref[4 * u + 2], skip_ref[4 * u + 3])
        skip_row = jnp.where(wide_lanes[:1] < PAIR, low_pair, high_pair)
        state = None
        offset = jnp.zeros((1, QUAD), F32)
        for q in range(subs):
            at = pl.ds(q * SUB, SUB)
            score = scores[g, q]
            intra, values, cums = [], [], []
            for p in range(2):
                cum0 = spread[at, 2 * p * SUB : (2 * p + 1) * SUB]
                cum1 = spread[at, (2 * p + 1) * SUB : (2 * p + 2) * SUB]
                row0 = cum_t[q, pl.ds(4 * u + 2 * p, 1), :]
                row1 = cum_t[q, pl.ds(4 * u + 2 * p + 1, 1), :]
                mix0 = score * jnp.exp2(jnp.minimum(cum0 - row0, 0.0))
                mix1 = score * jnp.exp2(jnp.minimum(cum1 - row1, 0.0))
                mix = jnp.concatenate([mix0.astype(BF16), mix1.astype(BF16)], axis=1)
                value32 = vbuf[2 * u + p, at, :].astype(F32)
                both = jnp.concatenate(
                    [
                        jnp.where(first_half, value32, 0.0).astype(BF16),
                        jnp.where(first_half, 0.0, value32).astype(BF16),
                    ],
                    axis=0,
                )
                intra.append(jnp.dot(mix, both, preferred_element_type=F32))
                values.append(value32)
                cums.append(jnp.where(first_half, cum0, cum1))
            value = jnp.concatenate(values, axis=1)
            cum_p = jnp.concatenate(cums, axis=1)
            total = jnp.concatenate(intra, axis=1) + skip_row * value
            end = cum_p[SUB - 1 :, :]
            decay = jnp.exp2(cum_p)
            if state is not None:
                total += decay * jnp.dot(
                    readout2[g, at, :], split_rows(state), preferred_element_type=F32
                )
            acc[u, at, :] = total
            dec[u, at, :] = decay * jnp.exp2(offset)
            scaled = (value * jnp.exp2(end - cum_p)).astype(BF16)
            here = jnp.dot(inputs_t[g, q], scaled, preferred_element_type=F32)
            state = here if state is None else jnp.exp2(end) * state + here
            offset = offset + end
        local[2 * u] = state[:, :PAIR]
        local[2 * u + 1] = state[:, PAIR:]
        final = jnp.exp2(offset)
        ending[2 * u] = jnp.broadcast_to(final[:, :PAIR], (8, PAIR))
        ending[2 * u + 1] = jnp.broadcast_to(final[:, PAIR:], (8, PAIR))

    def back_step(c):
        back_copy(own, c).wait_recv()
        bsend[c] = jnp.where(owner == me, own[c], brecv[c])

        @pl.when(me >= 2)
        def _():
            back_copy(bsend, c).start()

    relays = (me > 0) & (me < last)

    def carry_step(c):
        @pl.when(me == 1)
        def _():
            back_step(c)

        @pl.when(me > 0)
        def _():
            forward_copy(own, c).wait_recv()

        below = frecv[c]
        cached = jnp.where(owner == me, own[c], jnp.where(owner > me, bsend[c], below))
        carry = jnp.where(me == k, cached, below)

        @pl.when(relays)
        def _():
            onward = ending[c, :1, :] * carry + local[c]
            fsend[c] = jnp.where(me < k, cached, onward)
            forward_copy(fsend, c).start()

        local[c] = carry

    def finish(u):
        g = (2 * u) // pairs_per_group
        gate_copy(2 * u).wait()
        gate_copy(2 * u + 1).wait()
        carry = jnp.concatenate([local[2 * u], local[2 * u + 1]], axis=1)
        big[...] = jnp.dot(readout2[g], split_rows(carry), preferred_element_type=F32)
        for q in range(subs):
            at = pl.ds(q * SUB, SUB)
            summed = acc[u, at, :] + dec[u, at, :] * big[at, :]
            gate = jnp.concatenate([gbuf[2 * u, at, :], gbuf[2 * u + 1, at, :]], axis=1)
            half = 0.5 * gate.astype(F32)
            gated = summed * (half + half * jnp.tanh(half))
            squares[at, :] = (gated * gated).astype(BF16)
            acc[u, at, :] = gated
        big[...] = jnp.dot(squares[...], mean_of, preferred_element_type=F32)
        norm_row = jnp.concatenate(
            [norm_ref[pl.ds(2 * u, 1), :], norm_ref[pl.ds(2 * u + 1, 1), :]], axis=1
        )
        for q in range(subs):
            at = pl.ds(q * SUB, SUB)
            normed = (acc[u, at, :] * lax.rsqrt(big[at, :] + 1e-5) * norm_row).astype(BF16)
            obuf[2 * u, at, :] = normed[:, :PAIR]
            obuf[2 * u + 1, at, :] = normed[:, PAIR:]
        out_copy(2 * u).start()
        out_copy(2 * u + 1).start()

    units = pairs // 2
    carry_lag = jnp.where(relays, jnp.minimum(units, 2 * me - 1), 0)
    carry_lag = jnp.where(me == last, jnp.minimum(units, 2 * me - 2), carry_lag)
    finish_lag = jnp.where(relays, carry_lag + 2, carry_lag)

    @pl.loop(0, units + finish_lag)
    def _(step):
        @pl.when(step < units)
        def _():
            @pl.when(relays & (me >= 2))
            def _():
                back_step(2 * step)
                back_step(2 * step + 1)

            stage_one(step)

        @pl.when((step >= carry_lag) & (step < units + carry_lag))
        def _():
            carry_step(2 * (step - carry_lag))
            carry_step(2 * (step - carry_lag) + 1)

        @pl.when(step >= finish_lag)
        def _():
            finish(step - finish_lag)

    @pl.loop(0, pairs)
    def _(c):
        out_copy(c).wait()

        @pl.when(me >= 2)
        def _():
            back_copy(own, c).wait_send()

        @pl.when(me < last)
        def _():
            forward_copy(own, c).wait_send()


def on_device(
    n_seq,
    n_cache,
    head_values,
    gate_values,
    state_inputs,
    state_readout,
    log_decays,
    skip_gains,
    norm_gains,
    cached_states,
    owner_slots,
    prefix_blocks,
    prompt_sessions,
):
    _, block, width = head_values.shape
    heads = width // HEAD_DIM
    per_group = HEAD_COUNT // GROUPS
    groups = max(1, heads // per_group)
    pairs = heads // 2
    subs = block // SUB
    owned = cached_states.shape[0]
    cache_index = lax.axis_index("cache")

    def group_rows(array, which):
        rows = array[0, :, which]
        for index in range(1, n_cache):
            rows = jnp.where(
                cache_index == index, array[0, :, index * heads // per_group + which], rows
            )
        return rows

    inputs = [group_rows(state_inputs, g) for g in range(groups)]
    readout = [group_rows(state_readout, g) for g in range(groups)]
    smem = pl.BlockSpec(memory_space=pltpu.SMEM)
    vmem = pl.BlockSpec(memory_space=pltpu.VMEM)
    hbm = pl.BlockSpec(memory_space=pl.ANY)
    tiles = pltpu.VMEM((pairs, STATE, PAIR), F32)
    sems = pltpu.SemaphoreType.DMA((pairs,))
    out, live = pl.pallas_call(
        functools.partial(kernel, n_seq, pairs, pairs // groups, subs, owned),
        out_shape=(
            jax.ShapeDtypeStruct(head_values.shape, BF16),
            jax.ShapeDtypeStruct((1,), jnp.int32),
        ),
        in_specs=[smem] * 4 + [vmem] * (3 + 2 * groups) + [hbm] * 2,
        out_specs=(hbm, smem),
        scratch_shapes=[
            pltpu.VMEM((pairs, block, PAIR), BF16),
            pltpu.VMEM((pairs, block, PAIR), BF16),
            pltpu.VMEM((pairs, block, PAIR), BF16),
            pltpu.VMEM((pairs // 2, block, QUAD), F32),
            pltpu.VMEM((pairs // 2, block, QUAD), F32),
            tiles, tiles, tiles, tiles, tiles, tiles,
            pltpu.VMEM((pairs, 8, PAIR), F32),
            pltpu.VMEM((block, 128), BF16),
            pltpu.VMEM((subs, heads, SUB), F32),
            pltpu.VMEM((128, SUB), F32),
            pltpu.VMEM((groups, subs, SUB, SUB), F32),
            pltpu.VMEM((groups, subs, STATE, SUB), BF16),
            pltpu.VMEM((groups, block, 2 * STATE), BF16),
            pltpu.VMEM((block, 4 * SUB), F32),
            pltpu.VMEM((block, QUAD), F32),
            pltpu.VMEM((block, QUAD), BF16),
            sems, sems, sems, sems, sems, sems, sems,
        ],
        compiler_params=pltpu.CompilerParams(
            collective_id=0, has_side_effects=True, vmem_limit_bytes=58 * 1024 * 1024
        ),
        name="scan_chain",
    )(
        prompt_sessions, owner_slots, prefix_blocks, skip_gains,
        *inputs, *readout, log_decays[0].T, norm_gains.reshape(pairs, PAIR),
        cached_states.reshape(owned, pairs, PAIR, STATE), head_values, gate_values,
    )
    return jnp.where(live[0] > 0, out, jnp.zeros_like(out))


def solution(mesh):
    in_specs = (
        P("groups", "seq", ("head", "cache")),
        P("groups", "seq", ("head", "cache")),
        P("groups", "seq", "head", None),
        P("groups", "seq", "head", None),
        P("groups", "seq", ("head", "cache")),
        P(("head", "cache")),
        P(("head", "cache")),
        P(("groups", "seq"), ("head", "cache"), None, None),
        P("groups"),
        P("groups"),
        P("groups"),
    )
    return jax.shard_map(
        functools.partial(on_device, mesh.shape["seq"], mesh.shape["cache"]), mesh=mesh, in_specs=in_specs,
        out_specs=P("groups", "seq", ("head", "cache")), check_vma=False,
    )
```

time: 83.7 us -> 58.4 us (0.70)
  Pallas kernels: 71.8 us -> 44.5 us
  other arithmetic: 0 us -> 6.31 us
  local copies, waits for them, and re-layouts: 11.1 us -> 6.09 us
    pallas_call x1, Pallas kernels: 71.8 us -> 44.5 us  [on_device(): pl.pallas_call(functools.partial(kernel, n_seq, pairs, pairs // groups, s...]
    unnamed x2, local copies, waits for them, and re-layouts: 6.71 us -> 0.01 us
    select_n x0 -> x3, other arithmetic: none -> 6.31 us  [the longest x1 4.48 us: on_device(): return jnp.where(live[0] > 0, out, jnp.zeros_like(out))]
    slice x0 -> x2, local copies, waits for them, and re-layouts: none -> 6.09 us  [group_rows(): array[0, :, index * heads // per_group + which]]
    dynamic_slice x3 -> x0, local copies, waits for them, and re-layouts: 4.34 us -> none  [the longest x2 3.48 us: on_device(): lax.dynamic_slice_in_dim(state_readout, first, groups, 2)[0]]
where the time goes in v2:
time: 58.4 us; the launch traced here: 58.3 us
  Pallas kernels  44.5 us (76%)
  other arithmetic  6.31 us (11%)
  local copies, waits for them, and re-layouts  6.09 us (10%)
  between operations  1.39 us (2%)
    pallas_call x1, Pallas kernels, on_device(): pl.pallas_call(functools.partial(kernel, n_seq, pairs, pairs // groups, s...  44.5 us
    slice x2, local copies, waits for them, and re-layouts, group_rows(): array[0, :, index * heads // per_group + which]  6.09 us
    select_n x1, other arithmetic, on_device(): return jnp.where(live[0] > 0, out, jnp.zeros_like(out))  4.48 us
    select_n x2, other arithmetic, group_rows(): jnp.where(cache_index == index, array[0, :, index * heads // per_group +...  1.83 us

profile of v2, /device:TPU:24, one launch (start us, length us, event | category | flops | bytes accessed | tf_op | source)
XLA Modules:
  0.0 58.3 jit_solution(11937352414772335068)
XLA Ops:
  0.0 0.0 copy-start
  0.7 4.6 %fusion.5 = (bf16[1,1024,1,128]{3,2,1,0:T(2,128)(2,1)S(1)}, bf16[1,1024,1,128]{3,2,1,0:T(2,128)(2,1)S(1)}, bf16[1,1024,1,128]{3,2,1,0:T(2,128)(2,1)S(1)}, bf16[1,1024,1,128]{3,2,1,0:T(2,128)(2,1)S(1)}) fusion(bf16[1,1024,4,128]{3,2,1,0:T(4,128)(2,1)} %param.13), kind=kLoop, calls=%fused_computation.10 | loop fusion | bytes 2097152 | tf_op jit(solution)/shard_map/slice | solution.py:344
  5.3 0.9 %fusion.2 = (bf16[1024,128]{1,0:T(8,128)(2,1)}, bf16[1024,128]{1,0:T(8,128)(2,1)}) fusion(bf16[1,1024,1,128]{3,2,1,0:T(2,128)(2,1)S(1)} %get-tuple-element.16, bf16[1,1024,1,128]{3,2,1,0:T(2,128)(2,1)S(1)} %get-tuple-element.13, pred[]{:T(512)S(6)} %eq.2, bf16[1,1024,1,128]{3,2,1,0:T(2,128)(2,1)S(1)} %get-tuple-element.14, ...), kind=kLoop, calls=%fused_computation.6 | loop fusion | flops 262144 | bytes 1572865 | tf_op jit(solution)/shard_map/jit(_where)/select_n | solution.py:343
  6.2 0.0 copy-done
  6.2 1.5 %fusion.4 = (bf16[1,1024,1,128]{3,2,1,0:T(2,128)(2,1)S(1)}, bf16[1,1024,1,128]{3,2,1,0:T(2,128)(2,1)S(1)}, bf16[1,1024,1,128]{3,2,1,0:T(2,128)(2,1)S(1)}, bf16[1,1024,1,128]{3,2,1,0:T(2,128)(2,1)S(1)}) fusion(bf16[1,1024,4,128]{3,2,1,0:T(4,128)(2,1)S(1)} %copy-done), kind=kLoop, calls=%fused_computation.9 | loop fusion | bytes 2097152 | tf_op jit(solution)/shard_map/slice | solution.py:344
  7.8 0.9 %fusion = (bf16[1024,128]{1,0:T(8,128)(2,1)}, bf16[1024,128]{1,0:T(8,128)(2,1)}) fusion(bf16[1,1024,1,128]{3,2,1,0:T(2,128)(2,1)S(1)} %get-tuple-element.12, bf16[1,1024,1,128]{3,2,1,0:T(2,128)(2,1)S(1)} %get-tuple-element.9, pred[]{:T(512)S(6)} %eq.2, bf16[1,1024,1,128]{3,2,1,0:T(2,128)(2,1)S(1)} %get-tuple-element.10, ...), kind=kLoop, calls=%fused_computation.2 | loop fusion | flops 262144 | bytes 1572865 | tf_op jit(solution)/shard_map/jit(_where)/select_n | solution.py:343
  8.7 44.5 %scan_chain.1 = (bf16[1,1024,2048]{2,1,0:T(8,128)(2,1)}, s32[1]{0:T(128)}) custom-call(s32[1]{0:T(128)S(6)} %copy.44.sessions_ref, s32[8]{0:T(128)} %slots_ref.1, s32[8]{0:T(128)} %prefix_ref.1, f32[32]{0:T(128)} %skip_ref.1, bf16[1024,128]{1,0:T(8,128)(2,1)} %get-tuple-element.18.refs_0_, bf16[1024,128]{1,0:T(8,128)(2,1)} %get-tuple-element.17.refs_1_, ...), custom_call_target="tpu_custom_call" | custom-call | tf_op jit(solution)/shard_map/scan_chain/pallas_call | solution.py:355
  53.8 4.5 %broadcast_select_fusion = bf16[1,1024,2048]{2,1,0:T(8,128)(2,1)} fusion(bf16[1,1024,2048]{2,1,0:T(8,128)(2,1)} %get-tuple-element.8, pred[]{:T(512)} %bitcast.8), kind=kLoop, calls=%fused_computation | loop fusion | flops 2097152 | bytes 8388609 | tf_op jit(solution)/shard_map/jit(_where)/select_n | solution.py:391
Async XLA Ops:
  0.0 6.2 %copy-start = (bf16[1,1024,4,128]{3,2,1,0:T(4,128)(2,1)S(1)}, bf16[1,1024,4,128]{3,2,1,0:T(4,128)(2,1)}, u32[]{:S(2)}) copy-start(bf16[1,1024,4,128]{3,2,1,0:T(4,128)(2,1)} %param.14) | copy-start | bytes 3145732

commit v3 on v2

--- a/solution.py
+++ b/solution.py
@@ -27,20 +27,20 @@
 
 
 def kernel(
-    n_seq, pairs, pairs_per_group, subs, owned_rows,
+    n_seq, pairs, pairs_per_group, per_group, subs, owned_rows,
     sessions_ref, slots_ref, prefix_ref, skip_ref,
     *refs,
 ):
     me = lax.axis_index("seq")
     heads = 2 * pairs
     groups = pairs // pairs_per_group
-    inputs_refs, readout_refs = refs[:groups], refs[groups : 2 * groups]
+    first_group = lax.axis_index("cache") * heads // per_group
     (
-        decays_ref, norm_ref, cached_ref, values_hbm, gates_hbm, out_hbm, live_ref,
+        inputs_ref, readout_ref, decays_ref, norm_ref, cached_ref, values_hbm, gates_hbm, out_hbm, live_ref,
         vbuf, gbuf, obuf, acc, dec, own, bsend, brecv, fsend, frecv, local, ending,
-        cum3, cum_t, cum_pad, scores, inputs_t, readout2, spread, big, squares,
+        cum3, cum_t, cum_pad, scores, inputs_t, readout2, spread, big, squares, staged,
         vsem, gsem, osem, bsend_sem, brecv_sem, fsend_sem, frecv_sem,
-    ) = refs[2 * groups :]
+    ) = refs
     last = n_seq - 1
 
     def value_copy(c):
@@ -116,8 +116,10 @@
         @pl.when(me == 0)
         def _():
             bsend[c] = row
-            frecv[c] = row
-            forward_copy(own, c).start()
+            frecv[c] = jnp.zeros((STATE + 8, PAIR), F32)
+            fsend[c, :STATE, :] = row
+            fsend[c, STATE:, :] = jnp.zeros((8, PAIR), F32)
+            forward_copy(fsend, c).start()
 
     rows = lax.broadcasted_iota(jnp.int32, (SUB, SUB), 0)
     lanes = lax.broadcasted_iota(jnp.int32, (SUB, SUB), 1)
@@ -139,14 +141,19 @@
         cum3[at, :] = (
             high + pltpu.roll(middle, heads, axis=1) + pltpu.roll(low, 2 * heads, axis=1)
         ).astype(BF16)
+        for which, raw in enumerate((inputs_ref, readout_ref)):
+            staged[which] = raw[at].astype(F32).reshape(SUB * raw.shape[1], STATE)
+        step = inputs_ref.shape[1]
         for g in range(groups):
-            c_rows = readout_refs[g][at, :]
-            b_rows = inputs_refs[g][at, :]
+            mine = pl.ds(first_group + g, SUB, stride=step)
+            b_rows32 = staged[0, mine, :]
+            b_rows = b_rows32.astype(BF16)
+            c_rows = staged[1, mine, :].astype(BF16)
             product = lax.dot_general(
                 c_rows, b_rows, (((1,), (1,)), ((), ())), preferred_element_type=F32
             )
             scores[g, q] = jnp.where(causal, product, 0.0)
-            inputs_t[g, q] = b_rows.astype(F32).T.astype(BF16)
+            inputs_t[g, q] = b_rows32.T.astype(BF16)
             readout2[g, at, :] = jnp.concatenate([c_rows, c_rows], axis=1)
 
     wide_rows = lax.broadcasted_iota(jnp.int32, (QUAD, QUAD), 0)
@@ -229,31 +236,38 @@
     relays = (me > 0) & (me < last)
 
     def carry_step(c):
+        @pl.when(me > 0)
+        def _():
+            forward_copy(fsend, c).wait_recv()
+
+        below = frecv[c, :STATE, :]
+        factor = frecv[c, STATE:, :]
+
+        @pl.when(relays)
+        def _():
+            cached = jnp.where(owner == me, own[c], below)
+            added = jnp.where(owner == me, below + factor[:1] * own[c], below)
+            start = jnp.where(me == k, jnp.where(owner <= me, cached, 0.0), added)
+            onward = ending[c, :1, :] * start + local[c]
+            fsend[c, :STATE, :] = jnp.where(me < k, cached, onward)
+            fsend[c, STATE:, :] = ending[c] * jnp.where(me == k, 1.0, factor)
+            forward_copy(fsend, c).start()
+
+    def carry_of(c):
         @pl.when(me == 1)
         def _():
             back_step(c)
 
-        @pl.when(me > 0)
-        def _():
-            forward_copy(own, c).wait_recv()
-
-        below = frecv[c]
-        cached = jnp.where(owner == me, own[c], jnp.where(owner > me, bsend[c], below))
-        carry = jnp.where(me == k, cached, below)
-
-        @pl.when(relays)
-        def _():
-            onward = ending[c, :1, :] * carry + local[c]
-            fsend[c] = jnp.where(me < k, cached, onward)
-            forward_copy(fsend, c).start()
-
-        local[c] = carry
+        below = frecv[c, :STATE, :]
+        above = bsend[c]
+        later = jnp.where(owner >= me, below + frecv[c, STATE : STATE + 1, :] * above, below)
+        return jnp.where(me == k, jnp.where(owner >= me, above, below), later)
 
     def finish(u):
         g = (2 * u) // pairs_per_group
         gate_copy(2 * u).wait()
         gate_copy(2 * u + 1).wait()
-        carry = jnp.concatenate([local[2 * u], local[2 * u + 1]], axis=1)
+        carry = jnp.concatenate([carry_of(2 * u), carry_of(2 * u + 1)], axis=1)
         big[...] = jnp.dot(readout2[g], split_rows(carry), preferred_element_type=F32)
         for q in range(subs):
             at = pl.ds(q * SUB, SUB)
@@ -276,8 +290,7 @@
         out_copy(2 * u + 1).start()
 
     units = pairs // 2
-    carry_lag = jnp.where(relays, jnp.minimum(units, 2 * me - 1), 0)
-    carry_lag = jnp.where(me == last, jnp.minimum(units, 2 * me - 2), carry_lag)
+    carry_lag = jnp.minimum(units, jnp.where(me == last, me + 1, me))
     finish_lag = jnp.where(relays, carry_lag + 2, carry_lag)
 
     @pl.loop(0, units + finish_lag)
@@ -310,12 +323,11 @@
 
         @pl.when(me < last)
         def _():
-            forward_copy(own, c).wait_send()
+            forward_copy(fsend, c).wait_send()
 
 
 def on_device(
     n_seq,
-    n_cache,
     head_values,
     gate_values,
     state_inputs,
@@ -335,30 +347,19 @@
     pairs = heads // 2
     subs = block // SUB
     owned = cached_states.shape[0]
-    cache_index = lax.axis_index("cache")
-
-    def group_rows(array, which):
-        rows = array[0, :, which]
-        for index in range(1, n_cache):
-            rows = jnp.where(
-                cache_index == index, array[0, :, index * heads // per_group + which], rows
-            )
-        return rows
-
-    inputs = [group_rows(state_inputs, g) for g in range(groups)]
-    readout = [group_rows(state_readout, g) for g in range(groups)]
     smem = pl.BlockSpec(memory_space=pltpu.SMEM)
     vmem = pl.BlockSpec(memory_space=pltpu.VMEM)
     hbm = pl.BlockSpec(memory_space=pl.ANY)
+    sent = pltpu.VMEM((pairs, STATE + 8, PAIR), F32)
     tiles = pltpu.VMEM((pairs, STATE, PAIR), F32)
     sems = pltpu.SemaphoreType.DMA((pairs,))
     out, live = pl.pallas_call(
-        functools.partial(kernel, n_seq, pairs, pairs // groups, subs, owned),
+        functools.partial(kernel, n_seq, pairs, pairs // groups, per_group, subs, owned),
         out_shape=(
             jax.ShapeDtypeStruct(head_values.shape, BF16),
             jax.ShapeDtypeStruct((1,), jnp.int32),
         ),
-        in_specs=[smem] * 4 + [vmem] * (3 + 2 * groups) + [hbm] * 2,
+        in_specs=[smem] * 4 + [vmem] * 5 + [hbm] * 2,
         out_specs=(hbm, smem),
         scratch_shapes=[
             pltpu.VMEM((pairs, block, PAIR), BF16),
@@ -366,7 +367,7 @@
             pltpu.VMEM((pairs, block, PAIR), BF16),
             pltpu.VMEM((pairs // 2, block, QUAD), F32),
             pltpu.VMEM((pairs // 2, block, QUAD), F32),
-            tiles, tiles, tiles, tiles, tiles, tiles,
+            tiles, tiles, tiles, sent, sent, tiles,
             pltpu.VMEM((pairs, 8, PAIR), F32),
             pltpu.VMEM((block, 128), BF16),
             pltpu.VMEM((subs, heads, SUB), F32),
@@ -377,6 +378,7 @@
             pltpu.VMEM((block, 4 * SUB), F32),
             pltpu.VMEM((block, QUAD), F32),
             pltpu.VMEM((block, QUAD), BF16),
+            pltpu.VMEM((2, SUB * state_inputs.shape[2], STATE), F32),
             sems, sems, sems, sems, sems, sems, sems,
         ],
         compiler_params=pltpu.CompilerParams(
@@ -385,7 +387,7 @@
         name="scan_chain",
     )(
         prompt_sessions, owner_slots, prefix_blocks, skip_gains,
-        *inputs, *readout, log_decays[0].T, norm_gains.reshape(pairs, PAIR),
+        state_inputs[0], state_readout[0], log_decays[0].T, norm_gains.reshape(pairs, PAIR),
         cached_states.reshape(owned, pairs, PAIR, STATE), head_values, gate_values,
     )
     return jnp.where(live[0] > 0, out, jnp.zeros_like(out))
@@ -406,6 +408,6 @@
         P("groups"),
     )
     return jax.shard_map(
-        functools.partial(on_device, mesh.shape["seq"], mesh.shape["cache"]), mesh=mesh, in_specs=in_specs,
+        functools.partial(on_device, mesh.shape["seq"]), mesh=mesh, in_specs=in_specs,
         out_specs=P("groups", "seq", ("head", "cache")), check_vma=False,
     )

time: 58.4 us -> 49.3 us (0.84)
  local copies, waits for them, and re-layouts: 6.09 us -> 0 us
  other arithmetic: 6.31 us -> 4.48 us
  Pallas kernels: 44.5 us -> 43.4 us
    slice x2 -> x0, local copies, waits for them, and re-layouts: 6.09 us -> none  [group_rows(): array[0, :, index * heads // per_group + which]]
    select_n x2 -> x0, other arithmetic: 1.83 us -> none  [group_rows(): jnp.where(cache_index == index, array[0, :, index * heads // per_group +...]
    pallas_call x1, Pallas kernels: 44.5 us -> 43.4 us  [on_device(): pl.pallas_call(functools.partial(kernel, n_seq, pairs, pairs // groups, p...]
where the time goes in v3:
time: 49.3 us; the launch traced here: 49.1 us
  Pallas kernels  43.4 us (88%)
  other arithmetic  4.48 us (9%)
  between operations  1.27 us (3%)
    pallas_call x1, Pallas kernels, on_device(): pl.pallas_call(functools.partial(kernel, n_seq, pairs, pairs // groups, p...  43.4 us
    select_n x1, other arithmetic, on_device(): return jnp.where(live[0] > 0, out, jnp.zeros_like(out))  4.48 us

profile of v3, /device:TPU:24, one launch (start us, length us, event | category | flops | bytes accessed | tf_op | source)
XLA Modules:
  0.0 49.1 jit_solution(13311857303405385368)
XLA Ops:
  0.7 43.4 %scan_chain.1 = (bf16[1,1024,2048]{2,1,0:T(8,128)(2,1)}, s32[1]{0:T(128)}) custom-call(s32[1]{0:T(128)S(6)} %copy.12.sessions_ref, s32[8]{0:T(128)} %slots_ref.1, s32[8]{0:T(128)} %prefix_ref.1, f32[32]{0:T(128)} %skip_ref.1, bf16[1024,4,128]{2,1,0:T(4,128)(2,1)} %bitcast.9, bf16[1024,4,128]{2,1,0:T(4,128)(2,1)} %bitcast.10, f32[32,1024]{1,0:T(8,128)} %bitcast.11, ...), custom_call_target="tpu_custom_call" | custom-call | tf_op jit(solution)/shard_map/scan_chain/pallas_call | solution.py:356
  44.6 4.5 %broadcast_select_fusion = bf16[1,1024,2048]{2,1,0:T(8,128)(2,1)} fusion(bf16[1,1024,2048]{2,1,0:T(8,128)(2,1)} %get-tuple-element.8, pred[]{:T(512)} %bitcast.6), kind=kLoop, calls=%fused_computation | loop fusion | flops 2097152 | bytes 8388609 | tf_op jit(solution)/shard_map/jit(_where)/select_n | solution.py:393

commit v4 on v3

--- a/solution.py
+++ b/solution.py
@@ -291,7 +291,7 @@
 
     units = pairs // 2
     carry_lag = jnp.minimum(units, jnp.where(me == last, me + 1, me))
-    finish_lag = jnp.where(relays, carry_lag + 2, carry_lag)
+    finish_lag = jnp.where(relays, carry_lag + 4, carry_lag)
 
     @pl.loop(0, units + finish_lag)
     def _(step):

time: 49.3 us -> 49.3 us (level)
  no operation moved by 1% of the time
where the time goes in v4:
time: 49.3 us; the launch traced here: 49.1 us
  Pallas kernels  43.4 us (88%)
  other arithmetic  4.48 us (9%)
  between operations  1.27 us (3%)
    pallas_call x1, Pallas kernels, on_device(): pl.pallas_call(functools.partial(kernel, n_seq, pairs, pairs // groups, p...  43.4 us
    select_n x1, other arithmetic, on_device(): return jnp.where(live[0] > 0, out, jnp.zeros_like(out))  4.48 us

profile of v4, /device:TPU:24, one launch (start us, length us, event | category | flops | bytes accessed | tf_op | source)
XLA Modules:
  0.0 49.1 jit_solution(4906424079287668724)
XLA Ops:
  0.7 43.4 %scan_chain.1 = (bf16[1,1024,2048]{2,1,0:T(8,128)(2,1)}, s32[1]{0:T(128)}) custom-call(s32[1]{0:T(128)S(6)} %copy.12.sessions_ref, s32[8]{0:T(128)} %slots_ref.1, s32[8]{0:T(128)} %prefix_ref.1, f32[32]{0:T(128)} %skip_ref.1, bf16[1024,4,128]{2,1,0:T(4,128)(2,1)} %bitcast.9, bf16[1024,4,128]{2,1,0:T(4,128)(2,1)} %bitcast.10, f32[32,1024]{1,0:T(8,128)} %bitcast.11, ...), custom_call_target="tpu_custom_call" | custom-call | tf_op jit(solution)/shard_map/scan_chain/pallas_call | solution.py:356
  44.6 4.5 %broadcast_select_fusion = bf16[1,1024,2048]{2,1,0:T(8,128)(2,1)} fusion(bf16[1,1024,2048]{2,1,0:T(8,128)(2,1)} %get-tuple-element.8, pred[]{:T(512)} %bitcast.6), kind=kLoop, calls=%fused_computation | loop fusion | flops 2097152 | bytes 8388609 | tf_op jit(solution)/shard_map/jit(_where)/select_n | solution.py:393
